TPU v7x, 32 devices: a whole 2x2x4 slice. The times are simulated.
32 devices in a mesh: row: 8 (over z, y), col: 4 (over x, core).
Axes of the slice: x: 2, y: 2, z: 4, core: 2. Of those that a mesh axis runs over, the one named last changes fastest.
Arguments:
- tokens: bfloat16 [1600, 8192], P('row', 'col')
- ln1_gain: float32 [1600], P('row'), may hold values from 0.25 to 1.75
- ln1_shift: float32 [1600], P('row'), may hold values from -4 to 4
- weight_qkv: bfloat16 [1600, 4800], P('row', 'col'), may hold values from -0.21875 to 0.21875
- bias_qkv: float32 [4800], P('col'), may hold values from -4 to 4
- weight_out: bfloat16 [1600, 1600], P('row', 'col'), may hold values from -0.625 to 0.625
- bias_out: float32 [1600], P('row'), may hold values from -6 to 6
- ln2_gain: float32 [1600], P('row'), may hold values from 0.25 to 1.75
- ln2_shift: float32 [1600], P('row'), may hold values from -4 to 4
- weight_up: bfloat16 [1600, 6400], P('row', 'col'), may hold values from -0.15625 to 0.15625
- bias_up: float32 [6400], P('col'), may hold values from -6 to 6
- weight_down: bfloat16 [1600, 6400], P('row', 'col'), may hold values from -0.109375 to 0.109375
- bias_down: float32 [1600], P('row'), may hold values from -6 to 6
- cotangent: bfloat16 [1600, 8192], P('row', 'col')
Outputs:
- block_output: bfloat16 [1600, 8192], P('row', 'col')
- grad_tokens: float32 [1600, 8192], P('row', 'col')
- grad_ln1_gain: float32 [1600], P('row')
- grad_ln1_shift: float32 [1600], P('row')
- grad_weight_qkv: float32 [1600, 4800], P('row', 'col')
- grad_bias_qkv: float32 [4800], P('col')
- grad_weight_out: float32 [1600, 1600], P('row', 'col')
- grad_bias_out: float32 [1600], P('row')
- grad_ln2_gain: float32 [1600], P('row')
- grad_ln2_shift: float32 [1600], P('row')
- grad_weight_up: float32 [1600, 6400], P('row', 'col')
- grad_bias_up: float32 [6400], P('col')
- grad_weight_down: float32 [1600, 6400], P('row', 'col')
- grad_bias_down: float32 [1600], P('row')
All inputs are finite; a program needn't handle non-finite values.
Results may differ from a plain program's by a relative error of at most 0.012.
The roundings to bfloat16 on the way count: a program that leaves them out, or rounds other values in their place, can miss the bound.
Values may be sent and summed in bfloat16 or wider, within the bound.
A program may use at most 256 MiB of HBM per device.

v0:
```python
import jax
import jax.numpy as jnp
from jax import lax
from jax.sharding import PartitionSpec as P

D = 1600
H = 25
HD = 64
L = 1024
SEQ_ROW = 1
epsilon = 1e-05
excluded = -1e30


def row_totals(first_sum, second_sum):
    return lax.psum((first_sum, second_sum), "row")


def norm_forward(values, norm_gain, norm_shift):
    row_sum, row_squares = row_totals(jnp.sum(values, axis=0), jnp.sum(values * values, axis=0))
    row_mean = row_sum / D
    row_scale = lax.rsqrt(row_squares / D - row_mean * row_mean + epsilon)
    centred = (values - row_mean[None, :]) * row_scale[None, :]
    return (
        (centred * norm_gain[:, None] + norm_shift[:, None]).astype(jnp.bfloat16),
        centred,
        row_scale,
    )


def norm_backward(gradient, centred, row_scale, norm_gain):
    scaled = gradient * norm_gain[:, None]
    first_sum, second_sum = row_totals(jnp.sum(scaled, axis=0), jnp.sum(scaled * centred, axis=0))
    adjusted = scaled - first_sum[None, :] / D - centred * (second_sum[None, :] / D)
    return (
        adjusted * row_scale[None, :],
        jnp.sum(gradient * centred, axis=1),
        jnp.sum(gradient, axis=1),
    )


def spread_cols(values):
    return lax.all_gather(values, "col", axis=1, tiled=True)


def row_terms(gathered, weight):
    return lax.psum_scatter(
        lax.dot_general(
            gathered, weight, (((0,), (0,)), ((), ())), preferred_element_type=jnp.float32
        ),
        "row",
        scatter_dimension=0,
        tiled=True,
    )


def project_rows(gathered, weight):
    return row_terms(gathered, weight)


def share_cols(full_cols):
    return lax.psum_scatter(full_cols, "col", scatter_dimension=1, tiled=True)


def cross_products(values, weight):
    return share_cols(
        lax.dot_general(
            weight,
            lax.all_gather(values, "row", axis=0, tiled=True),
            (((1,), (1,)), ((), ())),
            preferred_element_type=jnp.float32,
        )
    )


def fold_rows(gradient, weight, gathered):

    def accumulate(running, block_rows, offset):
        through = lax.dot_general(
            weight, block_rows, (((1,), (1,)), ((), ())), preferred_element_type=jnp.float32
        )
        weight_grad = jnp.dot(gathered, block_rows, preferred_element_type=jnp.float32)
        return (through, weight_grad)

    initial = (
        jnp.zeros((weight.shape[0], gathered.shape[1]), jnp.float32),
        jnp.zeros(weight.shape, jnp.float32),
    )
    return accumulate(initial, lax.all_gather(gradient, "row", axis=0, tiled=True), jnp.int32(0))


def fold_again(values, gathered):

    def accumulate(running, block_rows, offset):
        return jnp.dot(gathered, block_rows, preferred_element_type=jnp.float32)

    initial = jnp.zeros((gathered.shape[0], values.shape[1]), jnp.float32)
    return accumulate(initial, lax.all_gather(values, "row", axis=0, tiled=True), jnp.int32(0))


def build_slots():
    col_count = lax.axis_size("col")
    unit_count = SEQ_ROW * H
    slot_count = (unit_count + col_count - 1) // col_count
    column_ids = jnp.arange(col_count, dtype=jnp.int32)[:, None]
    slot_ids = jnp.arange(slot_count, dtype=jnp.int32)[None, :]
    numbered = slot_ids * col_count + column_ids
    return jnp.where(numbered < unit_count, numbered, -1)


def slot_matrix(slot_table):
    return (
        slot_table.reshape(-1)[:, None] == jnp.arange(SEQ_ROW * H, dtype=jnp.int32)[None, :]
    ).astype(jnp.bfloat16)


def to_units(values, slot_table):
    channels = values.shape[1] // H
    by_unit = (
        values.reshape(SEQ_ROW, L, channels, H)
        .transpose(0, 3, 1, 2)
        .reshape(SEQ_ROW * H, L * channels)
    )
    outgoing = jnp.dot(slot_matrix(slot_table), by_unit, preferred_element_type=jnp.float32).astype(
        jnp.bfloat16
    )
    outgoing = outgoing.reshape(slot_table.shape[0], slot_table.shape[1], L, channels)
    return lax.all_to_all(outgoing, "col", split_axis=0, concat_axis=3, tiled=True)[0]


def to_tokens(unit_values, slot_table):
    returned = lax.all_to_all(unit_values[None], "col", split_axis=3, concat_axis=0, tiled=True)
    channels = returned.shape[3]
    flat = returned.reshape(slot_table.shape[0] * slot_table.shape[1], L * channels)
    placed = lax.dot_general(
        slot_matrix(slot_table), flat, (((0,), (0,)), ((), ())), preferred_element_type=jnp.float32
    )
    placed = placed.astype(jnp.bfloat16).reshape(SEQ_ROW, H, L, channels)
    return placed.transpose(0, 2, 3, 1).reshape(SEQ_ROW * L, channels * H)


def causal_mask():
    return jnp.arange(L)[:, None] >= jnp.arange(L)[None, :]


def attend_forward(unit_data):
    score_scale = HD ** (-0.5)
    allowed = causal_mask()

    def per_unit(unit_rows):
        query_rows = unit_rows[:, :HD]
        key_rows = unit_rows[:, HD : 2 * HD]
        value_rows = unit_rows[:, 2 * HD :]
        scores = (
            lax.dot_general(
                query_rows, key_rows, (((1,), (1,)), ((), ())), preferred_element_type=jnp.float32
            )
            * score_scale
        )
        scores = jnp.where(allowed, scores, excluded)
        peak = jnp.max(scores, axis=1, keepdims=True)
        weights = jnp.exp(scores - peak)
        row_total = jnp.sum(weights, axis=1, keepdims=True)
        weights_low = (weights / row_total).astype(jnp.bfloat16)
        attended = jnp.dot(weights_low, value_rows, preferred_element_type=jnp.float32).astype(
            jnp.bfloat16
        )
        return (attended, (peak + jnp.log(row_total))[:, 0])

    return lax.map(per_unit, unit_data)


def attend_backward(unit_data, grad_units, log_totals):
    score_scale = HD ** (-0.5)
    allowed = causal_mask()

    def per_unit(inputs):
        unit_rows, grad_rows, log_row = inputs
        query_rows = unit_rows[:, :HD]
        key_rows = unit_rows[:, HD : 2 * HD]
        value_rows = unit_rows[:, 2 * HD :]
        scores = (
            lax.dot_general(
                query_rows, key_rows, (((1,), (1,)), ((), ())), preferred_element_type=jnp.float32
            )
            * score_scale
        )
        scores = jnp.where(allowed, scores, excluded)
        weights = jnp.exp(scores - log_row[:, None])
        weights_low = weights.astype(jnp.bfloat16)
        grad_value = lax.dot_general(
            weights_low, grad_rows, (((0,), (0,)), ((), ())), preferred_element_type=jnp.float32
        )
        grad_weights = lax.dot_general(
            grad_rows, value_rows, (((1,), (1,)), ((), ())), preferred_element_type=jnp.float32
        )
        grad_scores = weights * (
            grad_weights - jnp.sum(weights * grad_weights, axis=1, keepdims=True)
        )
        grad_low = grad_scores.astype(jnp.bfloat16)
        grad_query = jnp.dot(grad_low, key_rows, preferred_element_type=jnp.float32) * score_scale
        grad_key = (
            lax.dot_general(
                grad_low, query_rows, (((0,), (0,)), ((), ())), preferred_element_type=jnp.float32
            )
            * score_scale
        )
        return jnp.concatenate([grad_query, grad_key, grad_value], axis=1).astype(jnp.bfloat16)

    return lax.map(per_unit, (unit_data, grad_units, log_totals))


def body(
    tokens,
    ln1_gain,
    ln1_shift,
    weight_qkv,
    bias_qkv,
    weight_out,
    bias_out,
    ln2_gain,
    ln2_shift,
    weight_up,
    bias_up,
    weight_down,
    bias_down,
    cotangent,
):
    slot_table = build_slots()
    residual_in = tokens.astype(jnp.float32)
    normed_in, centred_in, scale_in = norm_forward(residual_in, ln1_gain, ln1_shift)
    normed_wide = spread_cols(normed_in)
    qkv_rows = (project_rows(normed_wide, weight_qkv) + bias_qkv).astype(jnp.bfloat16)
    unit_data = to_units(qkv_rows, slot_table)
    attended_units, log_totals = attend_forward(unit_data)
    attended_rows = to_tokens(attended_units, slot_table)
    residual_mid = residual_in + cross_products(attended_rows, weight_out) + bias_out[:, None]
    normed_mid, centred_mid, scale_mid = norm_forward(residual_mid, ln2_gain, ln2_shift)
    mid_wide = spread_cols(normed_mid)
    hidden_pre = project_rows(mid_wide, weight_up) + bias_up
    hidden_rows = jax.nn.gelu(hidden_pre, approximate=True).astype(jnp.bfloat16)
    block_output = (
        residual_mid + cross_products(hidden_rows, weight_down) + bias_down[:, None]
    ).astype(jnp.bfloat16)
    grad_wide = spread_cols(cotangent)
    grad_bias_down = jnp.sum(grad_wide, axis=1, dtype=jnp.float32)
    grad_hidden = project_rows(grad_wide, weight_down)
    unused_value, gelu_back = jax.vjp(
        lambda inner: jax.nn.gelu(inner, approximate=True), hidden_pre
    )
    grad_pre = gelu_back(grad_hidden)[0].astype(jnp.bfloat16)
    up_part = jnp.sum(grad_pre, axis=0, dtype=jnp.float32)
    mid_full, grad_weight_up = fold_rows(grad_pre, weight_up, mid_wide)
    grad_normed_mid = share_cols(mid_full)
    grad_norm_mid, gain_two_part, shift_two_part = norm_backward(
        grad_normed_mid, centred_mid, scale_mid, ln2_gain
    )
    grad_residual_mid = cotangent.astype(jnp.float32) + grad_norm_mid
    grad_branch = grad_residual_mid.astype(jnp.bfloat16)
    branch_wide = spread_cols(grad_branch)
    grad_bias_out = jnp.sum(branch_wide, axis=1, dtype=jnp.float32)
    grad_attended = project_rows(branch_wide, weight_out).astype(jnp.bfloat16)
    grad_units = to_units(grad_attended, slot_table)
    grad_unit_qkv = attend_backward(unit_data, grad_units, log_totals)
    grad_qkv_rows = to_tokens(grad_unit_qkv, slot_table)
    qkv_part = jnp.sum(grad_qkv_rows, axis=0, dtype=jnp.float32)
    in_full, grad_weight_qkv = fold_rows(grad_qkv_rows, weight_qkv, normed_wide)
    grad_normed_in = share_cols(in_full)
    grad_norm_in, gain_one_part, shift_one_part = norm_backward(
        grad_normed_in, centred_in, scale_in, ln1_gain
    )
    grad_tokens = grad_residual_mid + grad_norm_in
    grad_weight_down = fold_again(hidden_rows, grad_wide)
    grad_weight_out = fold_again(attended_rows, branch_wide)
    grad_bias_up, grad_bias_qkv = lax.psum((up_part, qkv_part), "row")
    grad_ln1_gain, grad_ln1_shift, grad_ln2_gain, grad_ln2_shift = lax.psum(
        (gain_one_part, shift_one_part, gain_two_part, shift_two_part), "col"
    )
    return (
        block_output,
        grad_tokens,
        grad_ln1_gain,
        grad_ln1_shift,
        grad_weight_qkv,
        grad_bias_qkv,
        grad_weight_out,
        grad_bias_out,
        grad_ln2_gain,
        grad_ln2_shift,
        grad_weight_up,
        grad_bias_up,
        grad_weight_down,
        grad_bias_down,
    )


def solution(mesh):
    in_specs = (
        P("row", "col"),
        P("row"),
        P("row"),
        P("row", "col"),
        P("col"),
        P("row", "col"),
        P("row"),
        P("row"),
        P("row"),
        P("row", "col"),
        P("col"),
        P("row", "col"),
        P("row"),
        P("row", "col"),
    )
    out_specs = (
        P("row", "col"),
        P("row", "col"),
        P("row"),
        P("row"),
        P("row", "col"),
        P("col"),
        P("row", "col"),
        P("row"),
        P("row"),
        P("row"),
        P("row", "col"),
        P("col"),
        P("row", "col"),
        P("row"),
    )
    return jax.shard_map(body, mesh=mesh, in_specs=in_specs, out_specs=out_specs, check_vma=False)
```

profile of v0, /device:TPU:0, one launch (start us, length us, event | category | flops | bytes accessed | tf_op | source)
XLA Modules:
  0.0 4900.1 jit_solution(17613472183118926545)
XLA Ops:
  8.7 38.8 all-reduce.3
  50.7 26.6 all-gather.9.cloned.1.call-done
  77.3 17.4 fusion.69
  94.8 625.4 %reduce-scatter.9.cloned.1.call-done = f32[1024,1200]{0,1:T(8,128)} async-done(((f32[8192,1200]{0,1:T(8,128)}), f32[1024,1200]{0,1:T(8,128)}) %reduce-scatter.9.cloned.1.call-update) | async-done | bytes 4915216 | tf_op jit(solution)/shard_map/reduce_scatter | solution.py:47
  725.5 8.2 copy.41
  733.7 18.4 reshape.182
  756.7 9.4 reshape.183
  766.1 7.6 copy.42
  777.7 32.6 all-to-all-done
  818.2 51.8 %while.24 = (s32[]{:T(128)}, bf16[7,1024,64]{1,2,0:T(8,128)(2,1)S(1)}, f32[7,1024]{1,0:T(8,128)S(1)}, bf16[7,1024,192]{2,1,0:T(8,128)(2,1)}, s32[]{:T(128)}, /*index=5*/s32[]{:T(128)}) while((s32[]{:T(128)}, bf16[7,1024,64]{1,2,0:T(8,128)(2,1)S(1)}, f32[7,1024]{1,0:T(8,128)S(1)}, bf16[7,1024,192]{2,1,0:T(8,128)(2,1)}, s32[]{:T(128)}, ...), condition=%wide.region_8.9_spmd.clone, body=%wide.region_5.8_spmd.clone.sunk | while | flops 284228608 | bytes 30974060 | solution.py:170
  870.5 16.9 all_to_all.60
  892.6 16.8 reshape.184
  916.4 6.9 copy.47
  925.0 100.2 %all-gather.11.cloned.1.call-done = bf16[8192,400]{0,1:T(8,128)(2,1)} async-done(((bf16[1024,400]{0,1:T(8,128)(2,1)}), bf16[8192,400]{0,1:T(8,128)(2,1)}) %all-gather.11.cloned.1.call-update) | async-done | bytes 6553616 | tf_op jit(solution)/shard_map/all_gather | solution.py:69
  1025.2 7.5 convolution_bitcast_fusion.1
  1033.3 57.8 %reduce-scatter.11.cloned.1.call-done = f32[200,2048]{1,0:T(8,128)} async-done(((f32[200,8192]{1,0:T(8,128)}), f32[200,2048]{1,0:T(8,128)}) %reduce-scatter.11.cloned.1.call-update) | async-done | bytes 1638416 | tf_op jit(solution)/shard_map/reduce_scatter | solution.py:62
  1093.0 37.1 all-reduce.2
  1131.5 22.0 fusion.71
  1157.1 22.8 fusion.70
  1180.2 802.1 %reduce-scatter.17.cloned.1.call-done = f32[1024,1600]{0,1:T(8,128)} async-done(((f32[8192,1600]{0,1:T(8,128)}), f32[1024,1600]{0,1:T(8,128)}) %reduce-scatter.17.cloned.1.call-update) | async-done | bytes 6553616 | tf_op jit(solution)/shard_map/reduce_scatter | solution.py:47
  1982.3 824.9 %reduce-scatter.13.cloned.1.call-done = f32[1024,1600]{0,1:T(8,128)} async-done(((f32[8192,1600]{0,1:T(8,128)}), f32[1024,1600]{0,1:T(8,128)}) %reduce-scatter.13.cloned.1.call-update) | async-done | bytes 6553616 | tf_op jit(solution)/shard_map/reduce_scatter | solution.py:47
  2807.3 10.7 convert_reduce_fusion.2
  2818.1 499.3 %all-gather.19.cloned.1.call-done = bf16[8192,1600]{0,1:T(8,128)(2,1)} async-done(((bf16[1024,1600]{0,1:T(8,128)(2,1)}), bf16[8192,1600]{0,1:T(8,128)(2,1)}) %all-gather.19.cloned.1.call-update) | async-done | bytes 26214416 | tf_op jit(solution)/shard_map/all_gather | solution.py:89
  3317.4 13.3 convolution_bitcast_fusion.2
  3330.8 60.2 %reduce-scatter.19.cloned.1.call-done = f32[200,2048]{1,0:T(8,128)} async-done(((f32[200,8192]{1,0:T(8,128)}), f32[200,2048]{1,0:T(8,128)}) %reduce-scatter.19.cloned.1.call-update) | async-done | bytes 1638416 | tf_op jit(solution)/shard_map/reduce_scatter | solution.py:62
  3393.8 37.1 all-reduce.1
  3434.1 25.5 all-gather.21.cloned.1.call-done
  3459.6 8.5 fusion.72
  3468.2 215.1 %reduce-scatter.21.cloned.1.call-done = f32[1024,400]{0,1:T(8,128)} async-done(((f32[8192,400]{0,1:T(8,128)}), f32[1024,400]{0,1:T(8,128)}) %reduce-scatter.21.cloned.1.call-update) | async-done | bytes 1638416 | tf_op jit(solution)/shard_map/reduce_scatter | solution.py:47
  3690.5 16.6 reshape.188
  3707.6 6.9 reshape.189
  3725.0 12.7 all-to-all-done.2
  3737.8 49.8 %while.25 = (s32[]{:T(128)}, bf16[7,1024,192]{1,2,0:T(8,128)(2,1)}, bf16[7,1024,192]{2,1,0:T(8,128)(2,1)}, f32[7,1024]{1,0:T(8,128)S(1)}, bf16[7,1024,64]{1,2,0:T(8,128)(2,1)S(1)}, /*index=5*/s32[]{:T(128)}) while((s32[]{:T(128)}, bf16[7,1024,192]{1,2,0:T(8,128)(2,1)}, bf16[7,1024,192]{2,1,0:T(8,128)(2,1)}, ...), condition=%wide.region_25.26_spmd.clone, body=%wide.region_23.25_spmd.clone.sunk | while | flops 683080704 | bytes 34886228 | solution.py:210
  3790.9 40.7 all_to_all.61
  3831.6 8.3 copy.54
  3839.9 18.5 reshape.190
  3863.2 8.7 reshape.191
  3871.9 8.8 copy.55
  3886.1 374.8 %all-gather.23.cloned.1.call-done = bf16[8192,1200]{0,1:T(8,128)(2,1)} async-done(((bf16[1024,1200]{0,1:T(8,128)(2,1)}), bf16[8192,1200]{0,1:T(8,128)(2,1)}) %all-gather.23.cloned.1.call-update) | async-done | bytes 19660816 | tf_op jit(solution)/shard_map/all_gather | solution.py:89
  4260.8 13.9 convolution_bitcast_fusion
  4274.7 487.6 %all-gather.15.cloned.1.call-done = bf16[8192,1600]{0,1:T(8,128)(2,1)} async-done(((bf16[1024,1600]{0,1:T(8,128)(2,1)}), bf16[8192,1600]{0,1:T(8,128)(2,1)}) %all-gather.15.cloned.1.call-update) | async-done | bytes 26214416 | tf_op jit(solution)/shard_map/all_gather | solution.py:69
  4762.4 14.0 convolution_bitcast_fusion.3
  4779.8 15.1 convolution_bitcast_fusion.4
  4794.9 15.6 fusion.75
  4813.7 7.1 fusion.74
  4822.5 11.9 fusion.73
  4837.1 6.9 all-reduce.4
  4844.0 37.1 all-reduce
  (278 shorter events, 210.4 us)
Async XLA Ops:
  7.2 1149.9 %copy-start = (bf16[200,1600]{1,0:T(8,128)(2,1)S(1)}, bf16[200,1600]{1,0:T(8,128)(2,1)}, u32[]{:S(2)}) copy-start(bf16[200,1600]{1,0:T(8,128)(2,1)} %param.27) | copy-start | bytes 1920004
  7.2 70.1 %copy-start.12 = (bf16[200,1200]{1,0:T(8,128)(2,1)S(1)}, bf16[200,1200]{1,0:T(8,128)(2,1)}, u32[]{:S(2)}) copy-start(bf16[200,1200]{1,0:T(8,128)(2,1)} %param.21) | copy-start | bytes 1440004
  7.2 70.1 %all-gather.9.cloned.1.call-start = ((), (), s32[]{:S(2)}) async-start(), calls=%async_computation.12 | async-start | bytes 4096000 | tf_op jit(solution)/shard_map/all_gather | solution.py:43
  50.6 669.6 %reduce-scatter.9.cloned.1.call-start = ((), (), s32[]{:S(2)}) async-start(), calls=%async_computation.13 | async-start | bytes 44236800 | tf_op jit(solution)/shard_map/reduce_scatter | solution.py:47
  94.7 625.5 %copy-start.31 = (f32[1200]{0:T(1024)S(1)}, f32[1200]{0:T(1024)}, u32[]{:S(2)}) copy-start(f32[1200]{0:T(1024)} %param.22) | copy-start | bytes 14404
  773.7 36.6 all-to-all-start
  777.6 247.6 %all-gather.11.cloned.1.call-start = ((), (), s32[]{:S(2)}) async-start(), calls=%async_computation.14 | async-start | bytes 7372800 | tf_op jit(solution)/shard_map/all_gather | solution.py:69
  916.4 108.8 %copy-start.10 = (bf16[200,400]{1,0:T(8,128)(2,1)S(1)}, bf16[200,400]{1,0:T(8,128)(2,1)}, u32[]{:S(2)}) copy-start(bf16[200,400]{1,0:T(8,128)(2,1)} %param.23) | copy-start | bytes 480004
  924.5 166.6 %reduce-scatter.11.cloned.1.call-start = ((), (), s32[]{:S(2)}) async-start(), calls=%async_computation.15 | async-start | bytes 8192000 | tf_op jit(solution)/shard_map/reduce_scatter | solution.py:62
  1032.6 58.4 %copy-start.5 = (bf16[200,2048]{1,0:T(8,128)(2,1)S(1)}, bf16[200,2048]{1,0:T(8,128)(2,1)}, u32[]{:S(2)}) copy-start(bf16[200,2048]{1,0:T(8,128)(2,1)} %param.18) | copy-start | bytes 2457604
  1032.6 58.4 %copy-start.34 = (f32[200]{0:T(256)S(1)}, f32[200]{0:T(256)}, u32[]{:S(2)}) copy-start(f32[200]{0:T(256)} %param.24) | copy-start | bytes 2404
  1032.7 97.4 %copy-start.27 = (f32[200]{0:T(256)S(1)}, f32[200]{0:T(256)}, u32[]{:S(2)}) copy-start(f32[200]{0:T(256)} %param.25) | copy-start | bytes 2404
  1032.7 97.4 %copy-start.35 = (f32[200]{0:T(256)S(1)}, f32[200]{0:T(256)}, u32[]{:S(2)}) copy-start(f32[200]{0:T(256)} %param.26) | copy-start | bytes 2404
  1032.7 98.8 %all-gather.17.cloned.1.call-start = ((), (), s32[]{:S(2)}) async-start(), calls=%async_computation.20 | async-start | bytes 4096000 | tf_op jit(solution)/shard_map/all_gather | solution.py:43
  1033.3 123.8 %all-gather.13.cloned.1.call-start = ((), (), s32[]{:S(2)}) async-start(), calls=%async_computation.16 | async-start | bytes 4096000 | tf_op jit(solution)/shard_map/all_gather | solution.py:43
  1092.9 2337.9 %copy-start.3 = (f32[200,2048]{1,0:T(8,128)}, f32[200,2048]{1,0:T(8,128)S(1)}, u32[]{:S(2)}) copy-start(f32[200,2048]{1,0:T(8,128)S(1)} %get-tuple-element.163) | copy-start | bytes 4915204
  1130.1 2300.8 %copy-start.14 = (f32[2048]{0:T(1024)}, f32[2048]{0:T(1024)S(1)}, u32[]{:S(2)}) copy-start(f32[2048]{0:T(1024)S(1)} %get-tuple-element.171) | copy-start | bytes 24580
  1130.1 2300.8 %copy-start.16 = (f32[2048]{0:T(1024)}, f32[2048]{0:T(1024)S(1)}, u32[]{:S(2)}) copy-start(f32[2048]{0:T(1024)S(1)} %get-tuple-element.172) | copy-start | bytes 24580
  1131.4 851.0 %reduce-scatter.17.cloned.1.call-start = ((), (), s32[]{:S(2)}) async-start(), calls=%async_computation.21 | async-start | bytes 58982400 | tf_op jit(solution)/shard_map/reduce_scatter | solution.py:47
  1153.5 1653.8 %reduce-scatter.13.cloned.1.call-start = ((), (), s32[]{:S(2)}) async-start(), calls=%async_computation.17 | async-start | bytes 58982400 | tf_op jit(solution)/shard_map/reduce_scatter | solution.py:47
  1179.9 1627.3 %copy-start.30 = (f32[1600]{0:T(1024)S(1)}, f32[1600]{0:T(1024)}, u32[]{:S(2)}) copy-start(f32[1600]{0:T(1024)} %param.28) | copy-start | bytes 19204
  1180.0 2137.4 %all-gather.19.cloned.1.call-start = ((), (), s32[]{:S(2)}) async-start(), calls=%async_computation.22 | async-start | bytes 29491200 | tf_op jit(solution)/shard_map/all_gather | solution.py:89
  2818.0 572.9 %reduce-scatter.19.cloned.1.call-start = ((), (), s32[]{:S(2)}) async-start(), calls=%async_computation.23 | async-start | bytes 8192000 | tf_op jit(solution)/shard_map/reduce_scatter | solution.py:62
  3330.7 100.2 %copy-start.8 = (bf16[200,2048]{1,0:T(8,128)(2,1)S(1)}, bf16[200,2048]{1,0:T(8,128)(2,1)}, u32[]{:S(2)}) copy-start(bf16[200,2048]{1,0:T(8,128)(2,1)} %param.31) | copy-start | bytes 2457604
  3330.7 128.9 %all-gather.21.cloned.1.call-start = ((), (), s32[]{:S(2)}) async-start(), calls=%async_computation.24 | async-start | bytes 4096000 | tf_op jit(solution)/shard_map/all_gather | solution.py:43
  3430.9 37.3 copy-start.22
  3430.9 37.3 copy-start.24
  3433.9 249.4 %reduce-scatter.21.cloned.1.call-start = ((), (), s32[]{:S(2)}) async-start(), calls=%async_computation.25 | async-start | bytes 14745600 | tf_op jit(solution)/shard_map/reduce_scatter | solution.py:47
  3721.2 16.5 all-to-all-start.2
  3724.7 536.1 %all-gather.23.cloned.1.call-start = ((), (), s32[]{:S(2)}) async-start(), calls=%async_computation.26 | async-start | bytes 22118400 | tf_op jit(solution)/shard_map/all_gather | solution.py:89
  3885.2 375.6 %copy-start.13 = (bf16[200,1200]{1,0:T(8,128)(2,1)S(1)}, bf16[200,1200]{1,0:T(8,128)(2,1)}, u32[]{:S(2)}) copy-start(bf16[200,1200]{1,0:T(8,128)(2,1)} %param.21) | copy-start | bytes 1440004
  3885.3 877.1 %all-gather.15.cloned.1.call-start = ((), (), s32[]{:S(2)}) async-start(), calls=%async_computation.18 | async-start | bytes 29491200 | tf_op jit(solution)/shard_map/all_gather | solution.py:69
  3885.8 948.5 %reduce-scatter.23.cloned.1.call-start = ((), (), s32[]{:S(2)}) async-start(), calls=%async_computation.27 | async-start | bytes 8192000 | tf_op jit(solution)/shard_map/reduce_scatter | solution.py:62
  4274.7 487.7 %copy-start.11 = (bf16[200,1600]{1,0:T(8,128)(2,1)S(1)}, bf16[200,1600]{1,0:T(8,128)(2,1)}, u32[]{:S(2)}) copy-start(bf16[200,1600]{1,0:T(8,128)(2,1)} %param.29) | copy-start | bytes 1920004
  4274.7 612.9 %reduce-scatter.15.cloned.1.call-start = ((), (), s32[]{:S(2)}) async-start(), calls=%async_computation.19 | async-start | bytes 8192000 | tf_op jit(solution)/shard_map/reduce_scatter | solution.py:62
  4822.3 12.0 copy-start.6
  4822.3 12.0 copy-start.19
  4822.4 14.8 copy-start.32
  4822.4 14.8 copy-start.33
  4822.4 21.6 copy-start.26
  4822.4 65.2 %copy-start.15 = (f32[2048]{0:T(1024)S(1)}, f32[2048]{0:T(1024)}, u32[]{:S(2)}) copy-start(f32[2048]{0:T(1024)} %copy-done.14) | copy-start | bytes 24580
  4822.4 65.2 %copy-start.17 = (f32[2048]{0:T(1024)S(1)}, f32[2048]{0:T(1024)}, u32[]{:S(2)}) copy-start(f32[2048]{0:T(1024)} %copy-done.16) | copy-start | bytes 24580
  4822.4 65.2 %copy-start.23 = (f32[2048]{0:T(1024)S(1)}, f32[2048]{0:T(1024)}, u32[]{:S(2)}) copy-start(f32[2048]{0:T(1024)} %copy-done.22) | copy-start | bytes 24580
  4822.4 65.2 %copy-start.25 = (f32[2048]{0:T(1024)S(1)}, f32[2048]{0:T(1024)}, u32[]{:S(2)}) copy-start(f32[2048]{0:T(1024)} %copy-done.24) | copy-start | bytes 24580
  4822.4 65.2 %copy-start.28 = (f32[200]{0:T(256)S(1)}, f32[200]{0:T(256)}, u32[]{:S(2)}) copy-start(f32[200]{0:T(256)} %param.25) | copy-start | bytes 2404
  4822.4 65.2 %copy-start.36 = (f32[200]{0:T(256)S(1)}, f32[200]{0:T(256)}, u32[]{:S(2)}) copy-start(f32[200]{0:T(256)} %param.30) | copy-start | bytes 2404
  4834.3 53.3 %copy-start.4 = (f32[200,2048]{1,0:T(8,128)S(1)}, f32[200,2048]{1,0:T(8,128)}, u32[]{:S(2)}) copy-start(f32[200,2048]{1,0:T(8,128)} %copy-done.3) | copy-start | bytes 4915204
  4881.1 12.1 copy-start.1
  (15 other events, 65.8 us)
Sparse Core Ops, SparseCore 0:
  50.7 26.5 all-gather.8
  94.8 625.3 reduce-scatter.8
  924.6 100.4 all-gather.10
  1032.8 58.2 reduce-scatter.10
  1092.5 29.2 all-gather.16
  1131.5 25.5 all-gather.12
  1161.1 821.2 reduce-scatter.16
  1986.8 820.4 reduce-scatter.12
  2818.1 499.2 all-gather.18
  3330.8 60.0 reduce-scatter.18
  3434.0 25.5 all-gather.20
  3468.3 214.9 reduce-scatter.20
  3885.4 375.3 all-gather.22
  4262.3 500.0 all-gather.14
  4764.9 60.0 reduce-scatter.22
  4827.4 60.1 reduce-scatter.14
where the time goes:
time: 4910 us; the launch traced here: 4900 us
  waiting for transfers between devices  4160 us (85%)
  matrix products  234 us (5%)
  blocking collectives  215 us (4%)
  local copies, waits for them, and re-layouts  210 us (4%)
  other arithmetic  61.1 us (1%)
    reduce_scatter x4, waiting for transfers between devices, row_terms(): lax.psum_scatter(lax.dot_general(gathered, weight, (((0,), (0,)), ((), ()...  2470 us
    all_gather x2, waiting for transfers between devices, fold_rows(): lax.all_gather(gradient, 'row', axis=0, tiled=True)  874 us
    all_gather x2, waiting for transfers between devices, cross_products(): lax.all_gather(values, 'row', axis=0, tiled=True)  588 us
    psum x4, blocking collectives, row_totals(): return lax.psum((first_sum, second_sum), 'row')  150 us
    reduce_scatter x4, waiting for transfers between devices, share_cols(): return lax.psum_scatter(full_cols, 'col', scatter_dimension=1, tiled=True)  124 us
  transfers between devices with their start and end apart: 18, of which 16 were waited for; matrix products, arithmetic and copies ran while one was open for 3% of the time, Pallas kernels for 0%

commit v1 on v0

--- a/solution.py
+++ b/solution.py
@@ -10,6 +10,19 @@
 SEQ_ROW = 1
 epsilon = 1e-05
 excluded = -1e30
+
+
+def ring_gather(array, axis, dim):
+    size, mine, width = (lax.axis_size(axis), lax.axis_index(axis), array.shape[dim])
+    upward = [(i, (i + 1) % size) for i in range(size)]
+    result = jnp.zeros((*array.shape[:dim], size * width, *array.shape[dim + 1 :]), array.dtype)
+    block = array
+    for step in range(size):
+        owner = (mine - step) % size
+        result = lax.dynamic_update_slice_in_dim(result, block, owner * width, axis=dim)
+        if step < size - 1:
+            block = lax.ppermute(block, axis, upward)
+    return result
 
 
 def row_totals(first_sum, second_sum):
@@ -66,7 +79,7 @@
     return share_cols(
         lax.dot_general(
             weight,
-            lax.all_gather(values, "row", axis=0, tiled=True),
+            ring_gather(values, "row", 0),
             (((1,), (1,)), ((), ())),
             preferred_element_type=jnp.float32,
         )

time: 4910 us -> 5590 us (1.14)
  waiting for transfers between devices: 4160 us -> 4790 us
    ppermute x0 -> x14, waiting for transfers between devices: none -> 698 us  [ring_gather(): block = lax.ppermute(block, axis, upward)]
    all_gather x2, waiting for transfers between devices: 588 us -> 503 us  [fold_again(): lax.all_gather(values, 'row', axis=0, tiled=True)]
  transfers between devices with their start and end apart: 18 -> 32, of which waited for: 16 -> 30; matrix products, arithmetic and copies ran while one was open for 3% -> 3% of each run, Pallas kernels for 0% -> 0%
where the time goes in v1:
time: 5590 us; the launch traced here: 5570 us
  waiting for transfers between devices  4790 us (86%)
  local copies, waits for them, and re-layouts  233 us (4%)
  blocking collectives  215 us (4%)
  matrix products  215 us (4%)
  other arithmetic  69.2 us (1%)
    reduce_scatter x4, waiting for transfers between devices, row_terms(): lax.psum_scatter(lax.dot_general(gathered, weight, (((0,), (0,)), ((), ()...  2470 us
    all_gather x2, waiting for transfers between devices, fold_rows(): lax.all_gather(gradient, 'row', axis=0, tiled=True)  849 us
    ppermute x14, waiting for transfers between devices, ring_gather(): block = lax.ppermute(block, axis, upward)  698 us
    all_gather x2, waiting for transfers between devices, fold_again(): lax.all_gather(values, 'row', axis=0, tiled=True)  503 us
    reduce_scatter x4, waiting for transfers between devices, share_cols(): return lax.psum_scatter(full_cols, 'col', scatter_dimension=1, tiled=True)  172 us
    psum x4, blocking collectives, row_totals(): return lax.psum((first_sum, second_sum), 'row')  151 us
  transfers between devices with their start and end apart: 32, of which 30 were waited for; matrix products, arithmetic and copies ran while one was open for 3% of the time, Pallas kernels for 0%

profile of v1, /device:TPU:0, one launch (start us, length us, event | category | flops | bytes accessed | tf_op | source)
XLA Modules:
  0.0 5574.5 jit_solution(8702668828624583694)
XLA Ops:
  8.7 38.8 all-reduce.3
  50.6 26.6 all-gather.9.cloned.1.call-done
  77.2 16.9 fusion.69
  94.2 625.6 %reduce-scatter.9.cloned.1.call-done = f32[1024,1200]{0,1:T(8,128)} async-done(((f32[8192,1200]{0,1:T(8,128)}), f32[1024,1200]{0,1:T(8,128)}) %reduce-scatter.9.cloned.1.call-update) | async-done | bytes 4915216 | tf_op jit(solution)/shard_map/reduce_scatter | solution.py:60
  733.4 18.4 reshape.182
  777.4 32.6 all-to-all-done
  817.9 22.8 while.24
  841.2 16.9 all_to_all.60
  863.3 16.8 reshape.184
  895.8 20.8 collective-permute-done
  916.7 21.4 collective-permute-done.1
  938.1 20.5 collective-permute-done.2
  959.4 19.6 collective-permute-done.3
  979.9 18.7 collective-permute-done.4
  998.6 18.0 collective-permute-done.5
  1039.5 59.0 %reduce-scatter.11.cloned.1.call-done = f32[200,2048]{1,0:T(8,128)} async-done(((f32[200,8192]{1,0:T(8,128)}), f32[200,2048]{1,0:T(8,128)}) %reduce-scatter.11.cloned.1.call-update) | async-done | bytes 1638416 | tf_op jit(solution)/shard_map/reduce_scatter | solution.py:75
  1100.4 37.1 all-reduce.2
  1138.9 22.0 fusion.71
  1164.6 22.8 fusion.70
  1187.6 801.8 %reduce-scatter.17.cloned.1.call-done = f32[1024,1600]{0,1:T(8,128)} async-done(((f32[8192,1600]{0,1:T(8,128)}), f32[1024,1600]{0,1:T(8,128)}) %reduce-scatter.17.cloned.1.call-update) | async-done | bytes 6553616 | tf_op jit(solution)/shard_map/reduce_scatter | solution.py:60
  1989.5 824.9 %reduce-scatter.13.cloned.1.call-done = f32[1024,1600]{0,1:T(8,128)} async-done(((f32[8192,1600]{0,1:T(8,128)}), f32[1024,1600]{0,1:T(8,128)}) %reduce-scatter.13.cloned.1.call-update) | async-done | bytes 6553616 | tf_op jit(solution)/shard_map/reduce_scatter | solution.py:60
  2824.5 499.3 %all-gather.15.cloned.1.call-done = bf16[8192,1600]{0,1:T(8,128)(2,1)} async-done(((bf16[1024,1600]{0,1:T(8,128)(2,1)}), bf16[8192,1600]{0,1:T(8,128)(2,1)}) %all-gather.15.cloned.1.call-update) | async-done | bytes 26214416 | tf_op jit(solution)/shard_map/all_gather | solution.py:102
  3323.8 13.3 convolution_bitcast_fusion.2
  3337.3 60.2 %reduce-scatter.19.cloned.1.call-done = f32[200,2048]{1,0:T(8,128)} async-done(((f32[200,8192]{1,0:T(8,128)}), f32[200,2048]{1,0:T(8,128)}) %reduce-scatter.19.cloned.1.call-update) | async-done | bytes 1638416 | tf_op jit(solution)/shard_map/reduce_scatter | solution.py:75
  3400.3 37.1 all-reduce.1
  3440.7 25.5 all-gather.17.cloned.1.call-done
  3474.7 215.1 %reduce-scatter.21.cloned.1.call-done = f32[1024,400]{0,1:T(8,128)} async-done(((f32[8192,400]{0,1:T(8,128)}), f32[1024,400]{0,1:T(8,128)}) %reduce-scatter.21.cloned.1.call-update) | async-done | bytes 1638416 | tf_op jit(solution)/shard_map/reduce_scatter | solution.py:60
  3697.3 16.6 reshape.188
  3744.6 49.9 while.25
  3797.8 40.7 all_to_all.61
  3846.9 18.6 reshape.190
  3909.2 121.7 %collective-permute-done.7 = bf16[1024,1600]{0,1:T(8,128)(2,1)} collective-permute-done((bf16[1024,1600]{0,1:T(8,128)(2,1)}, bf16[1024,1600]{0,1:T(8,128)(2,1)}, u32[]{:S(2)}, u32[]{:S(2)}) %collective-permute-start.7) | collective-permute-done | bytes 3276832 | tf_op jit(solution)/shard_map/ppermute | solution.py:24
  4030.9 93.6 %collective-permute-done.8 = bf16[1024,1600]{0,1:T(8,128)(2,1)S(1)} collective-permute-done((bf16[1024,1600]{0,1:T(8,128)(2,1)}, bf16[1024,1600]{0,1:T(8,128)(2,1)S(1)}, u32[]{:S(2)}, u32[]{:S(2)}) %collective-permute-start.8) | collective-permute-done | bytes 3276832 | tf_op jit(solution)/shard_map/ppermute | solution.py:24
  4128.7 74.6 %collective-permute-done.9 = bf16[1024,1600]{0,1:T(8,128)(2,1)} collective-permute-done((bf16[1024,1600]{0,1:T(8,128)(2,1)S(1)}, bf16[1024,1600]{0,1:T(8,128)(2,1)}, u32[]{:S(2)}, u32[]{:S(2)}) %collective-permute-start.9) | collective-permute-done | bytes 3276832 | tf_op jit(solution)/shard_map/ppermute | solution.py:24
  4203.3 16.0 collective-permute-start.10
  4219.3 349.2 %all-gather.19.cloned.1.call-done = bf16[8192,1200]{0,1:T(8,128)(2,1)} async-done(((bf16[1024,1200]{0,1:T(8,128)(2,1)}), bf16[8192,1200]{0,1:T(8,128)(2,1)}) %all-gather.19.cloned.1.call-update) | async-done | bytes 19660816 | tf_op jit(solution)/shard_map/all_gather | solution.py:102
  4568.6 13.8 convolution_bitcast_fusion
  4585.4 146.5 %collective-permute-done.11 = bf16[1024,1600]{0,1:T(8,128)(2,1)S(1)} collective-permute-done((bf16[1024,1600]{0,1:T(8,128)(2,1)}, bf16[1024,1600]{0,1:T(8,128)(2,1)S(1)}, u32[]{:S(2)}, u32[]{:S(2)}) %collective-permute-start.11) | collective-permute-done | bytes 3276832 | tf_op jit(solution)/shard_map/ppermute | solution.py:24
  4734.4 73.4 %collective-permute-done.12 = bf16[1024,1600]{0,1:T(8,128)(2,1)S(1)} collective-permute-done((bf16[1024,1600]{0,1:T(8,128)(2,1)S(1)}, bf16[1024,1600]{0,1:T(8,128)(2,1)S(1)}, u32[]{:S(2)}, u32[]{:S(2)}) %collective-permute-start.12) | collective-permute-done | bytes 3276832 | tf_op jit(solution)/shard_map/ppermute | solution.py:24
  4825.8 56.7 %collective-permute-done.13 = bf16[1024,1600]{0,1:T(8,128)(2,1)S(1)} collective-permute-done((bf16[1024,1600]{0,1:T(8,128)(2,1)S(1)}, bf16[1024,1600]{0,1:T(8,128)(2,1)S(1)}, u32[]{:S(2)}, u32[]{:S(2)}) %collective-permute-start.13) | collective-permute-done | bytes 3276832 | tf_op jit(solution)/shard_map/ppermute | solution.py:24
  4884.6 13.7 convolution_bitcast_fusion.3
  4901.4 430.6 %all-gather.23.cloned.1.call-done = bf16[8192,1600]{0,1:T(8,128)(2,1)} async-done(((bf16[1024,1600]{0,1:T(8,128)(2,1)}), bf16[8192,1600]{0,1:T(8,128)(2,1)}) %all-gather.23.cloned.1.call-update) | async-done | bytes 26214416 | tf_op jit(solution)/shard_map/all_gather | solution.py:111
  5332.0 15.2 convolution_bitcast_fusion.4
  5347.2 15.5 fusion.75
  5365.8 72.7 %all-gather.21.cloned.1.call-done = bf16[8192,400]{0,1:T(8,128)(2,1)} async-done(((bf16[1024,400]{0,1:T(8,128)(2,1)}), bf16[8192,400]{0,1:T(8,128)(2,1)}) %all-gather.21.cloned.1.call-update) | async-done | bytes 6553616 | tf_op jit(solution)/shard_map/all_gather | solution.py:111
  5462.8 36.6 reduce-scatter.23.cloned.1.call-done
  5508.0 37.9 all-reduce
  5545.9 16.0 reduce-scatter.15.cloned.1.call-done
  (315 shorter events, 369.5 us)
Async XLA Ops:
  7.2 1157.4 %copy-start = (bf16[200,1600]{1,0:T(8,128)(2,1)S(1)}, bf16[200,1600]{1,0:T(8,128)(2,1)}, u32[]{:S(2)}) copy-start(bf16[200,1600]{1,0:T(8,128)(2,1)} %param.27) | copy-start | bytes 1920004
  7.2 70.1 %all-gather.9.cloned.1.call-start = ((), (), s32[]{:S(2)}) async-start(), calls=%async_computation.12 | async-start | bytes 4096000 | tf_op jit(solution)/shard_map/all_gather | solution.py:56
  50.6 669.3 %reduce-scatter.9.cloned.1.call-start = ((), (), s32[]{:S(2)}) async-start(), calls=%async_computation.13 | async-start | bytes 44236800 | tf_op jit(solution)/shard_map/reduce_scatter | solution.py:60
  94.1 625.7 %copy-start.35 = (f32[1200]{0:T(1024)S(1)}, f32[1200]{0:T(1024)}, u32[]{:S(2)}) copy-start(f32[1200]{0:T(1024)} %param.22) | copy-start | bytes 14404
  773.7 36.4 all-to-all-start
  777.3 321.2 %reduce-scatter.11.cloned.1.call-start = ((), (), s32[]{:S(2)}) async-start(), calls=%async_computation.14 | async-start | bytes 8192000 | tf_op jit(solution)/shard_map/reduce_scatter | solution.py:75
  894.3 123.6 %copy-start.6 = (bf16[1024,400]{0,1:T(8,128)(2,1)}, bf16[1024,400]{0,1:T(8,128)(2,1)S(1)}, u32[]{:S(2)}) copy-start(bf16[1024,400]{0,1:T(8,128)(2,1)S(1)} %reshape.186) | copy-start | bytes 2457604
  894.3 22.4 collective-permute-start
  916.7 21.4 collective-permute-start.1
  938.1 20.5 collective-permute-start.2
  959.4 19.6 collective-permute-start.3
  979.9 18.7 collective-permute-start.4
  998.6 18.0 collective-permute-start.5
  1016.7 17.4 collective-permute-start.6
  1038.9 100.0 %all-gather.13.cloned.1.call-start = ((), (), s32[]{:S(2)}) async-start(), calls=%async_computation.18 | async-start | bytes 4096000 | tf_op jit(solution)/shard_map/all_gather | solution.py:56
  1039.5 125.1 %all-gather.11.cloned.1.call-start = ((), (), s32[]{:S(2)}) async-start(), calls=%async_computation.15 | async-start | bytes 4096000 | tf_op jit(solution)/shard_map/all_gather | solution.py:56
  1100.4 2337.0 %copy-start.2 = (f32[200,2048]{1,0:T(8,128)}, f32[200,2048]{1,0:T(8,128)S(1)}, u32[]{:S(2)}) copy-start(f32[200,2048]{1,0:T(8,128)S(1)} %get-tuple-element.165) | copy-start | bytes 4915204
  1137.5 2299.9 %copy-start.18 = (f32[2048]{0:T(1024)}, f32[2048]{0:T(1024)S(1)}, u32[]{:S(2)}) copy-start(f32[2048]{0:T(1024)S(1)} %get-tuple-element.172) | copy-start | bytes 24580
  1137.5 2299.9 %copy-start.20 = (f32[2048]{0:T(1024)}, f32[2048]{0:T(1024)S(1)}, u32[]{:S(2)}) copy-start(f32[2048]{0:T(1024)S(1)} %get-tuple-element.173) | copy-start | bytes 24580
  1138.8 850.6 %reduce-scatter.17.cloned.1.call-start = ((), (), s32[]{:S(2)}) async-start(), calls=%async_computation.19 | async-start | bytes 58982400 | tf_op jit(solution)/shard_map/reduce_scatter | solution.py:60
  1160.9 1653.5 %reduce-scatter.13.cloned.1.call-start = ((), (), s32[]{:S(2)}) async-start(), calls=%async_computation.16 | async-start | bytes 58982400 | tf_op jit(solution)/shard_map/reduce_scatter | solution.py:60
  1187.4 1627.0 %copy-start.31 = (f32[1600]{0:T(1024)S(1)}, f32[1600]{0:T(1024)}, u32[]{:S(2)}) copy-start(f32[1600]{0:T(1024)} %param.28) | copy-start | bytes 19204
  1187.4 2136.4 %all-gather.15.cloned.1.call-start = ((), (), s32[]{:S(2)}) async-start(), calls=%async_computation.20 | async-start | bytes 29491200 | tf_op jit(solution)/shard_map/all_gather | solution.py:102
  2824.5 573.0 %reduce-scatter.19.cloned.1.call-start = ((), (), s32[]{:S(2)}) async-start(), calls=%async_computation.21 | async-start | bytes 8192000 | tf_op jit(solution)/shard_map/reduce_scatter | solution.py:75
  3337.2 128.9 %all-gather.17.cloned.1.call-start = ((), (), s32[]{:S(2)}) async-start(), calls=%async_computation.22 | async-start | bytes 4096000 | tf_op jit(solution)/shard_map/all_gather | solution.py:56
  3440.4 249.4 %reduce-scatter.21.cloned.1.call-start = ((), (), s32[]{:S(2)}) async-start(), calls=%async_computation.23 | async-start | bytes 14745600 | tf_op jit(solution)/shard_map/reduce_scatter | solution.py:60
  3728.0 16.5 all-to-all-start.2
  3731.5 837.1 %all-gather.19.cloned.1.call-start = ((), (), s32[]{:S(2)}) async-start(), calls=%async_computation.24 | async-start | bytes 22118400 | tf_op jit(solution)/shard_map/all_gather | solution.py:102
  3892.2 1439.8 %all-gather.23.cloned.1.call-start = ((), (), s32[]{:S(2)}) async-start(), calls=%async_computation.27 | async-start | bytes 29491200 | tf_op jit(solution)/shard_map/all_gather | solution.py:111
  3901.3 667.2 %copy-start.17 = (bf16[200,1200]{1,0:T(8,128)(2,1)S(1)}, bf16[200,1200]{1,0:T(8,128)(2,1)}, u32[]{:S(2)}) copy-start(bf16[200,1200]{1,0:T(8,128)(2,1)} %param.21) | copy-start | bytes 1440004
  3907.6 1531.0 %all-gather.21.cloned.1.call-start = ((), (), s32[]{:S(2)}) async-start(), calls=%async_computation.26 | async-start | bytes 7372800 | tf_op jit(solution)/shard_map/all_gather | solution.py:111
  3907.6 123.3 %collective-permute-start.7 = (bf16[1024,1600]{0,1:T(8,128)(2,1)}, bf16[1024,1600]{0,1:T(8,128)(2,1)}, u32[]{:S(2)}, u32[]{:S(2)}) collective-permute-start(bf16[1024,1600]{0,1:T(8,128)(2,1)} %get-tuple-element.164), channel_id=1, source_target_pairs={{0,4},{4,8},{8,12},{12,16},{16,20},{20,24},{24,28},{28,0},{1,5},{5... | collective-permute-start | bytes 9830408 | tf_op jit(solution)/shard_map/ppermute | solution.py:24
  3909.2 1590.2 %reduce-scatter.23.cloned.1.call-start = ((), (), s32[]{:S(2)}) async-start(), calls=%async_computation.25 | async-start | bytes 8192000 | tf_op jit(solution)/shard_map/reduce_scatter | solution.py:75
  4030.9 93.6 %collective-permute-start.8 = (bf16[1024,1600]{0,1:T(8,128)(2,1)}, bf16[1024,1600]{0,1:T(8,128)(2,1)S(1)}, u32[]{:S(2)}, u32[]{:S(2)}) collective-permute-start(bf16[1024,1600]{0,1:T(8,128)(2,1)} %collective-permute-done.7), channel_id=1, source_target_pairs={{0,4},{4,8},{8,12},{12,16},{16,20},{20,24},{24,28},{28,0},{1,5},{5... | collective-permute-start | bytes 9830408 | tf_op jit(solution)/shard_map/ppermute | solution.py:24
  4126.3 77.0 %collective-permute-start.9 = (bf16[1024,1600]{0,1:T(8,128)(2,1)S(1)}, bf16[1024,1600]{0,1:T(8,128)(2,1)}, u32[]{:S(2)}, u32[]{:S(2)}) collective-permute-start(bf16[1024,1600]{0,1:T(8,128)(2,1)S(1)} %collective-permute-done.8), channel_id=1, source_target_pairs={{0,4},{4,8},{8,12},{12,16},{16,20},{20,24},{24,28},{28,0},{1,5},{5... | collective-permute-start | bytes 9830408 | tf_op jit(solution)/shard_map/ppermute | solution.py:24
  4203.3 379.1 %collective-permute-start.10 = (bf16[1024,1600]{0,1:T(8,128)(2,1)}, bf16[1024,1600]{0,1:T(8,128)(2,1)}, u32[]{:S(2)}, u32[]{:S(2)}) collective-permute-start(bf16[1024,1600]{0,1:T(8,128)(2,1)} %collective-permute-done.9), channel_id=1, source_target_pairs={{0,4},{4,8},{8,12},{12,16},{16,20},{20,24},{24,28},{28,0},{1,5},{5... | collective-permute-start | bytes 9830408 | tf_op jit(solution)/shard_map/ppermute | solution.py:24
  4582.4 979.5 %reduce-scatter.15.cloned.1.call-start = ((), (), s32[]{:S(2)}) async-start(), calls=%async_computation.17 | async-start | bytes 8192000 | tf_op jit(solution)/shard_map/reduce_scatter | solution.py:75
  4582.4 229.3 %copy-start.9 = (bf16[1024,1600]{0,1:T(8,128)(2,1)S(1)}, bf16[1024,1600]{0,1:T(8,128)(2,1)}, u32[]{:S(2)}) copy-start(bf16[1024,1600]{0,1:T(8,128)(2,1)} %copy-done.8) | copy-start | bytes 9830404
  4582.4 149.5 %collective-permute-start.11 = (bf16[1024,1600]{0,1:T(8,128)(2,1)}, bf16[1024,1600]{0,1:T(8,128)(2,1)S(1)}, u32[]{:S(2)}, u32[]{:S(2)}) collective-permute-start(bf16[1024,1600]{0,1:T(8,128)(2,1)} %collective-permute-done.10), channel_id=1, source_target_pairs={{0,4},{4,8},{8,12},{12,16},{16,20},{20,24},{24,28},{28,0},{1,5},{5... | collective-permute-start | bytes 9830408 | tf_op jit(solution)/shard_map/ppermute | solution.py:24
  4732.0 75.7 %collective-permute-start.12 = (bf16[1024,1600]{0,1:T(8,128)(2,1)S(1)}, bf16[1024,1600]{0,1:T(8,128)(2,1)S(1)}, u32[]{:S(2)}, u32[]{:S(2)}) collective-permute-start(bf16[1024,1600]{0,1:T(8,128)(2,1)S(1)} %collective-permute-done.11), channel_id=1, source_target_pairs={{0,4},{4,8},{8,12},{12,16},{16,20},{20,24},{24,28},{28,0},{1,5},{5... | collective-permute-start | bytes 9830408 | tf_op jit(solution)/shard_map/ppermute | solution.py:24
  4807.7 74.8 %collective-permute-start.13 = (bf16[1024,1600]{0,1:T(8,128)(2,1)S(1)}, bf16[1024,1600]{0,1:T(8,128)(2,1)S(1)}, u32[]{:S(2)}, u32[]{:S(2)}) collective-permute-start(bf16[1024,1600]{0,1:T(8,128)(2,1)S(1)} %collective-permute-done.12), channel_id=1, source_target_pairs={{0,4},{4,8},{8,12},{12,16},{16,20},{20,24},{24,28},{28,0},{1,5},{5... | collective-permute-start | bytes 9830408 | tf_op jit(solution)/shard_map/ppermute | solution.py:24
  5450.5 111.4 %copy-start.3 = (f32[200,2048]{1,0:T(8,128)S(1)}, f32[200,2048]{1,0:T(8,128)}, u32[]{:S(2)}) copy-start(f32[200,2048]{1,0:T(8,128)} %copy-done.2) | copy-start | bytes 4915204
  5450.5 111.4 %copy-start.19 = (f32[2048]{0:T(1024)S(1)}, f32[2048]{0:T(1024)}, u32[]{:S(2)}) copy-start(f32[2048]{0:T(1024)} %copy-done.18) | copy-start | bytes 24580
  5450.5 111.4 %copy-start.21 = (f32[2048]{0:T(1024)S(1)}, f32[2048]{0:T(1024)}, u32[]{:S(2)}) copy-start(f32[2048]{0:T(1024)} %copy-done.20) | copy-start | bytes 24580
  5450.5 111.4 %copy-start.27 = (f32[2048]{0:T(1024)S(1)}, f32[2048]{0:T(1024)}, u32[]{:S(2)}) copy-start(f32[2048]{0:T(1024)} %copy-done.26) | copy-start | bytes 24580
  5450.5 111.4 %copy-start.29 = (f32[2048]{0:T(1024)S(1)}, f32[2048]{0:T(1024)}, u32[]{:S(2)}) copy-start(f32[2048]{0:T(1024)} %copy-done.28) | copy-start | bytes 24580
  5450.5 111.4 %copy-start.33 = (f32[200]{0:T(256)S(1)}, f32[200]{0:T(256)}, u32[]{:S(2)}) copy-start(f32[200]{0:T(256)} %param.25) | copy-start | bytes 2404
  5450.5 111.4 %copy-start.40 = (f32[200]{0:T(256)S(1)}, f32[200]{0:T(256)}, u32[]{:S(2)}) copy-start(f32[200]{0:T(256)} %param.30) | copy-start | bytes 2404
  (25 other events, 975.2 us)
Sparse Core Ops, SparseCore 0:
  50.7 26.5 all-gather.8
  94.2 625.5 reduce-scatter.8
  1039.0 59.4 reduce-scatter.10
  1099.9 29.2 all-gather.12
  1138.9 25.5 all-gather.10
  1168.3 821.0 reduce-scatter.16
  1993.9 820.4 reduce-scatter.12
  2824.6 499.2 all-gather.14
  3337.3 60.0 reduce-scatter.18
  3440.5 25.5 all-gather.16
  3474.8 214.9 reduce-scatter.20
  3892.3 676.2 all-gather.18
  4570.2 761.8 all-gather.22
  5334.3 104.1 all-gather.20
  5441.1 58.2 reduce-scatter.22
  5501.7 60.1 reduce-scatter.14
